TPU v7x, 256 devices: a whole 4x4x8 slice. The times are simulated.
256 devices in a mesh: rows: 16 (over y, x), keys: 16 (over z, core).
Axes of the slice: x: 4, y: 4, z: 8, core: 2. Of those that a mesh axis runs over, the one named last changes fastest.
Arguments:
- pair_rep: bfloat16 [768, 768, 128], P('rows', 'keys'), may hold values from -6 to 6
- norm_gain: float32 [128], replicated, may hold values from 0.1 to 1.9
- w_query: bfloat16 [128, 128], replicated, may hold values from -0.5 to 0.5
- w_key: bfloat16 [128, 128], replicated, may hold values from -0.5 to 0.5
- w_value: bfloat16 [128, 128], replicated, may hold values from -0.5 to 0.5
- w_gate: bfloat16 [128, 128], replicated, may hold values from -0.5 to 0.5
- w_out: bfloat16 [128, 128], replicated, may hold values from -0.5 to 0.5
- pair_bias: bfloat16 [4, 768, 768], P(None, 'keys', 'rows'), may hold values from -12 to 300
Outputs:
- update: bfloat16 [768, 768, 128], P('rows', 'keys')
All inputs are finite; a program needn't handle non-finite values.
Results may differ from a plain program's by a relative error of at most 0.025.
Values may be sent and summed in bfloat16 or wider, within the bound.
A program may use at most 128 MiB of HBM per device.

v0:
```python
import jax
import jax.numpy as jnp
from jax import lax
from jax.sharding import Mesh
from jax.sharding import PartitionSpec as P

ROWS = ("rows_0", "rows_1")


epsilon = 1e-05
block_rows = 8


def gathered_by_axis(array, axes, dim):
    out = array
    for number in range(len(axes) - 1, -1, -1):
        out = lax.all_gather(out, axes[number], axis=dim, tiled=True)
    return out


def normalize(pair_rep, norm_gain):
    values = pair_rep.astype(jnp.float32)
    center = jnp.mean(values, axis=-1, keepdims=True)
    spread = jnp.mean(jnp.square(values - center), axis=-1, keepdims=True)
    return ((values - center) * lax.rsqrt(spread + epsilon) * norm_gain).astype(jnp.bfloat16)


def split_heads(tensor, head_count):
    return tensor.reshape(tensor.shape[:-1] + (head_count, tensor.shape[-1] // head_count))


def blocked(tensor):
    return tensor.reshape((tensor.shape[0] // block_rows, block_rows) + tensor.shape[1:])


def unblocked(tensor):
    return tensor.reshape((tensor.shape[0] * tensor.shape[1],) + tensor.shape[2:])


def absorb(running, query_block, key_block, value_block, bias_piece, head_count):
    highest, totals, summed = running
    logits = (
        jnp.einsum(
            "rjhd,rkhd->rhjk",
            split_heads(query_block, head_count),
            split_heads(key_block, head_count),
            preferred_element_type=jnp.float32,
        )
        + bias_piece.astype(jnp.float32)[None]
    )
    new_highest = jnp.maximum(highest, jnp.max(logits, axis=3))
    shrink = jnp.exp(highest - new_highest)
    powers = jnp.exp(logits - new_highest[..., None])
    totals = totals * shrink + jnp.sum(powers, axis=3)
    summed = summed * jnp.transpose(shrink, (0, 2, 1))[..., None] + jnp.einsum(
        "rhjk,rkhd->rjhd",
        powers.astype(jnp.bfloat16),
        split_heads(value_block, head_count),
        preferred_element_type=jnp.float32,
    )
    return (new_highest, totals, summed)


def body(pair_rep, norm_gain, w_query, w_key, w_value, w_gate, w_out, pair_bias):
    head_count = pair_bias.shape[0]
    inner_width = w_query.shape[1]
    normed = normalize(pair_rep, norm_gain)
    local_rows, local_keys = (normed.shape[0], normed.shape[1])
    queries = (
        jnp.dot(normed, w_query, preferred_element_type=jnp.float32)
        * (inner_width // head_count) ** (-0.5)
    ).astype(jnp.bfloat16)
    gates = jax.nn.sigmoid(jnp.dot(normed, w_gate, preferred_element_type=jnp.float32))
    bias_full = gathered_by_axis(pair_bias, ROWS, 2)
    initial = (
        jnp.full((local_rows, head_count, local_keys), -1e30, jnp.float32),
        jnp.zeros((local_rows, head_count, local_keys), jnp.float32),
        jnp.zeros((local_rows, local_keys, head_count, inner_width // head_count), jnp.float32),
    )
    piece = lax.all_gather(normed, "keys", axis=1, tiled=True)

    def one_block(arrays):
        highest, totals, summed, query_block, input_block = arrays
        key_block = jnp.dot(input_block, w_key, preferred_element_type=jnp.float32).astype(
            jnp.bfloat16
        )
        value_block = jnp.dot(input_block, w_value, preferred_element_type=jnp.float32).astype(
            jnp.bfloat16
        )
        return absorb(
            (highest, totals, summed), query_block, key_block, value_block, bias_full, head_count
        )

    results = lax.map(one_block, tuple((blocked(tensor) for tensor in initial + (queries, piece))))
    highest, totals, summed = tuple((unblocked(tensor) for tensor in results))
    attended = summed / jnp.transpose(totals, (0, 2, 1))[..., None]
    attended = attended.reshape(local_rows, local_keys, inner_width)
    gated = (gates * attended).astype(jnp.bfloat16)
    return jnp.dot(gated, w_out, preferred_element_type=jnp.float32).astype(jnp.bfloat16)


def solution(mesh):
    torus = Mesh(mesh.devices.reshape(4, 4, mesh.shape["keys"]), ("rows_0", "rows_1", "keys"))
    placed = (P(ROWS, "keys", None), P(), P(), P(), P(), P(), P(), P(None, "keys", ROWS))
    return jax.shard_map(
        body, mesh=torus, in_specs=placed, out_specs=P(ROWS, "keys", None), check_vma=False
    )
```

profile of v0, /device:TPU:1, one launch (start us, length us, event | category | flops | bytes accessed | tf_op | source)
XLA Modules:
  0.0 142.0 jit_solution(230207090936119171)
XLA Ops:
  9.9 2.2 %fusion.37 = bf16[48,48,128]{2,1,0:T(8,128)(2,1)} fusion(bf16[48,48,128]{2,1,0:T(8,128)(2,1)S(1)} %copy-done.1, f32[128]{0:T(128)} %param.11, f32[48,48]{1,0:T(8,128)S(1)} %add_rsqrt_fusion, f32[48,48]{1,0:T(8,128)S(1)} %broadcast_multiply_fusion), kind=kLoop, calls=%fused_computation.41 | loop fusion | flops 1474560 | bytes 1198592 | tf_op jit(solution)/shard_map/convert_element_type | solution.py:25
  12.4 10.5 %all_gather.10 = bf16[4,48,192]{1,0,2:T(4,128)(2,1)S(1)} all-gather(bf16[4,48,48]{1,0,2:T(4,128)(2,1)S(1)} %copy.25), channel_id=1, replica_groups=mesh['rows_0'=4,'rows_1'=4,'keys'=16] {'rows_1'}, dimensions={2}, use_global_device_ids=true | all-gather | bytes 92160 | tf_op jit(solution)/shard_map/all_gather | solution.py:17
  22.8 12.1 %all_gather.11 = bf16[4,48,768]{1,0,2:T(4,128)(2,1)S(1)} all-gather(bf16[4,48,192]{1,0,2:T(4,128)(2,1)S(1)} %all_gather.10), channel_id=1, replica_groups=mesh['rows_0'=4,'rows_1'=4,'keys'=16] {'rows_0'}, dimensions={2}, use_global_device_ids=true | all-gather | bytes 368640 | tf_op jit(solution)/shard_map/all_gather | solution.py:17
  35.9 41.3 %all-gather.2.cloned.1.call-done = bf16[48,768,128]{2,1,0:T(8,128)(2,1)} async-done(((bf16[48,48,128]{2,1,0:T(8,128)(2,1)}), bf16[48,768,128]{2,1,0:T(8,128)(2,1)}) %all-gather.2.cloned.1.call-update) | async-done | bytes 9437200 | tf_op jit(solution)/shard_map/all_gather | solution.py:80
  77.2 49.3 %while.12 = (s32[]{:T(128)}, f32[6,8,4,48]{3,2,1,0:T(4,128)S(1)}, f32[6,8,48,4,32]{2,4,3,1,0:T(8,128)}, bf16[6,8,48,128]{3,2,1,0:T(8,128)(2,1)S(1)}, bf16[6,8,76...) while((s32[]{:T(128)}, f32[6,8,4,48]{3,2,1,0:T(4,128)S(1)}, ...), condition=%wide.region_5.6_spmd, body=%wide.region_2.5_spmd.sunk | while | flops 564862464 | bytes 27426936 | solution.py:94
  77.5 2.0 %convolution_convert_fusion.5 = bf16[8,768,128]{1,2,0:T(8,128)(2,1)S(1)} fusion(bf16[6,8,768,128]{3,2,1,0:T(8,128)(2,1)} %get-tuple-element.181, s32[]{:T(128)S(6)} %copy.40, bf16[128,128]{0,1:T(8,128)(2,1)S(1)} %get-tuple-element.182), kind=kOutput, calls=%fused_computation.8.clone.1 | convolution fusion | flops 202113024 | bytes 3178500 | tf_op jit(solution)/shard_map/while/body/eval_jaxpr/dot_general | solution.py:84
  81.6 2.0 %convolution_convert_fusion.6 = bf16[8,768,128]{1,2,0:T(8,128)(2,1)S(1)} fusion(bf16[6,8,768,128]{3,2,1,0:T(8,128)(2,1)} %get-tuple-element.181, s32[]{:T(128)S(6)} %copy.40, bf16[128,128]{0,1:T(8,128)(2,1)S(1)} %get-tuple-element.184), kind=kOutput, calls=%fused_computation.7.clone.1 | convolution fusion | flops 202113024 | bytes 3178500 | tf_op jit(solution)/shard_map/while/body/eval_jaxpr/dot_general | solution.py:87
  83.6 1.9 %fusion.71 = f32[6,8,48,4,32]{2,4,3,1,0:T(8,128)} fusion(f32[6,8,48,4,32]{2,4,3,1,0:T(8,128)} %get-tuple-element.170, s32[]{:T(128)S(6)} %copy.40, bf16[8,768,4,32]{1,3,2,0:T(8,128)(2,1)S(1)} %bitcast.81, f32[8,4,48,768]{3,2,1,0:T(8,128)S(1)} %get-tuple-element.155, f32[8,4,48]{2,1,0:T(4,128)S(1)} %get-tuple-element.157, ...), kind=kOutput, calls=%fused_computation.16.clone.1 | convolution fusion | flops 79085568 | bytes 7417860 | tf_op jit(solution)/shard_map/while/body/eval_jaxpr/rhjk,rkhd->rjhd/dot_general | solution.py:55
  85.7 2.0 %convolution_convert_fusion.5 = bf16[8,768,128]{1,2,0:T(8,128)(2,1)S(1)} fusion(bf16[6,8,768,128]{3,2,1,0:T(8,128)(2,1)} %get-tuple-element.181, s32[]{:T(128)S(6)} %copy.40, bf16[128,128]{0,1:T(8,128)(2,1)S(1)} %get-tuple-element.182), kind=kOutput, calls=%fused_computation.8.clone.1 | convolution fusion | flops 202113024 | bytes 3178500 | tf_op jit(solution)/shard_map/while/body/eval_jaxpr/dot_general | solution.py:84
  89.8 2.0 %convolution_convert_fusion.6 = bf16[8,768,128]{1,2,0:T(8,128)(2,1)S(1)} fusion(bf16[6,8,768,128]{3,2,1,0:T(8,128)(2,1)} %get-tuple-element.181, s32[]{:T(128)S(6)} %copy.40, bf16[128,128]{0,1:T(8,128)(2,1)S(1)} %get-tuple-element.184), kind=kOutput, calls=%fused_computation.7.clone.1 | convolution fusion | flops 202113024 | bytes 3178500 | tf_op jit(solution)/shard_map/while/body/eval_jaxpr/dot_general | solution.py:87
  93.9 2.0 %convolution_convert_fusion.5 = bf16[8,768,128]{1,2,0:T(8,128)(2,1)S(1)} fusion(bf16[6,8,768,128]{3,2,1,0:T(8,128)(2,1)} %get-tuple-element.181, s32[]{:T(128)S(6)} %copy.40, bf16[128,128]{0,1:T(8,128)(2,1)S(1)} %get-tuple-element.182), kind=kOutput, calls=%fused_computation.8.clone.1 | convolution fusion | flops 202113024 | bytes 3178500 | tf_op jit(solution)/shard_map/while/body/eval_jaxpr/dot_general | solution.py:84
  98.0 2.0 %convolution_convert_fusion.6 = bf16[8,768,128]{1,2,0:T(8,128)(2,1)S(1)} fusion(bf16[6,8,768,128]{3,2,1,0:T(8,128)(2,1)} %get-tuple-element.181, s32[]{:T(128)S(6)} %copy.40, bf16[128,128]{0,1:T(8,128)(2,1)S(1)} %get-tuple-element.184), kind=kOutput, calls=%fused_computation.7.clone.1 | convolution fusion | flops 202113024 | bytes 3178500 | tf_op jit(solution)/shard_map/while/body/eval_jaxpr/dot_general | solution.py:87
  100.0 1.9 %fusion.71 = f32[6,8,48,4,32]{2,4,3,1,0:T(8,128)} fusion(f32[6,8,48,4,32]{2,4,3,1,0:T(8,128)} %get-tuple-element.170, s32[]{:T(128)S(6)} %copy.40, bf16[8,768,4,32]{1,3,2,0:T(8,128)(2,1)S(1)} %bitcast.81, f32[8,4,48,768]{3,2,1,0:T(8,128)S(1)} %get-tuple-element.155, f32[8,4,48]{2,1,0:T(4,128)S(1)} %get-tuple-element.157, ...), kind=kOutput, calls=%fused_computation.16.clone.1 | convolution fusion | flops 79085568 | bytes 7417860 | tf_op jit(solution)/shard_map/while/body/eval_jaxpr/rhjk,rkhd->rjhd/dot_general | solution.py:55
  102.1 2.0 %convolution_convert_fusion.5 = bf16[8,768,128]{1,2,0:T(8,128)(2,1)S(1)} fusion(bf16[6,8,768,128]{3,2,1,0:T(8,128)(2,1)} %get-tuple-element.181, s32[]{:T(128)S(6)} %copy.40, bf16[128,128]{0,1:T(8,128)(2,1)S(1)} %get-tuple-element.182), kind=kOutput, calls=%fused_computation.8.clone.1 | convolution fusion | flops 202113024 | bytes 3178500 | tf_op jit(solution)/shard_map/while/body/eval_jaxpr/dot_general | solution.py:84
  106.2 2.0 %convolution_convert_fusion.6 = bf16[8,768,128]{1,2,0:T(8,128)(2,1)S(1)} fusion(bf16[6,8,768,128]{3,2,1,0:T(8,128)(2,1)} %get-tuple-element.181, s32[]{:T(128)S(6)} %copy.40, bf16[128,128]{0,1:T(8,128)(2,1)S(1)} %get-tuple-element.184), kind=kOutput, calls=%fused_computation.7.clone.1 | convolution fusion | flops 202113024 | bytes 3178500 | tf_op jit(solution)/shard_map/while/body/eval_jaxpr/dot_general | solution.py:87
  108.2 1.9 %fusion.71 = f32[6,8,48,4,32]{2,4,3,1,0:T(8,128)} fusion(f32[6,8,48,4,32]{2,4,3,1,0:T(8,128)} %get-tuple-element.170, s32[]{:T(128)S(6)} %copy.40, bf16[8,768,4,32]{1,3,2,0:T(8,128)(2,1)S(1)} %bitcast.81, f32[8,4,48,768]{3,2,1,0:T(8,128)S(1)} %get-tuple-element.155, f32[8,4,48]{2,1,0:T(4,128)S(1)} %get-tuple-element.157, ...), kind=kOutput, calls=%fused_computation.16.clone.1 | convolution fusion | flops 79085568 | bytes 7417860 | tf_op jit(solution)/shard_map/while/body/eval_jaxpr/rhjk,rkhd->rjhd/dot_general | solution.py:55
  110.4 2.0 %convolution_convert_fusion.5 = bf16[8,768,128]{1,2,0:T(8,128)(2,1)S(1)} fusion(bf16[6,8,768,128]{3,2,1,0:T(8,128)(2,1)} %get-tuple-element.181, s32[]{:T(128)S(6)} %copy.40, bf16[128,128]{0,1:T(8,128)(2,1)S(1)} %get-tuple-element.182), kind=kOutput, calls=%fused_computation.8.clone.1 | convolution fusion | flops 202113024 | bytes 3178500 | tf_op jit(solution)/shard_map/while/body/eval_jaxpr/dot_general | solution.py:84
  114.5 2.0 %convolution_convert_fusion.6 = bf16[8,768,128]{1,2,0:T(8,128)(2,1)S(1)} fusion(bf16[6,8,768,128]{3,2,1,0:T(8,128)(2,1)} %get-tuple-element.181, s32[]{:T(128)S(6)} %copy.40, bf16[128,128]{0,1:T(8,128)(2,1)S(1)} %get-tuple-element.184), kind=kOutput, calls=%fused_computation.7.clone.1 | convolution fusion | flops 202113024 | bytes 3178500 | tf_op jit(solution)/shard_map/while/body/eval_jaxpr/dot_general | solution.py:87
  118.6 2.0 %convolution_convert_fusion.5 = bf16[8,768,128]{1,2,0:T(8,128)(2,1)S(1)} fusion(bf16[6,8,768,128]{3,2,1,0:T(8,128)(2,1)} %get-tuple-element.181, s32[]{:T(128)S(6)} %copy.40, bf16[128,128]{0,1:T(8,128)(2,1)S(1)} %get-tuple-element.182), kind=kOutput, calls=%fused_computation.8.clone.1 | convolution fusion | flops 202113024 | bytes 3178500 | tf_op jit(solution)/shard_map/while/body/eval_jaxpr/dot_general | solution.py:84
  122.7 2.0 %convolution_convert_fusion.6 = bf16[8,768,128]{1,2,0:T(8,128)(2,1)S(1)} fusion(bf16[6,8,768,128]{3,2,1,0:T(8,128)(2,1)} %get-tuple-element.181, s32[]{:T(128)S(6)} %copy.40, bf16[128,128]{0,1:T(8,128)(2,1)S(1)} %get-tuple-element.184), kind=kOutput, calls=%fused_computation.7.clone.1 | convolution fusion | flops 202113024 | bytes 3178500 | tf_op jit(solution)/shard_map/while/body/eval_jaxpr/dot_general | solution.py:87
  124.7 1.9 %fusion.71 = f32[6,8,48,4,32]{2,4,3,1,0:T(8,128)} fusion(f32[6,8,48,4,32]{2,4,3,1,0:T(8,128)} %get-tuple-element.170, s32[]{:T(128)S(6)} %copy.40, bf16[8,768,4,32]{1,3,2,0:T(8,128)(2,1)S(1)} %bitcast.81, f32[8,4,48,768]{3,2,1,0:T(8,128)S(1)} %get-tuple-element.155, f32[8,4,48]{2,1,0:T(4,128)S(1)} %get-tuple-element.157, ...), kind=kOutput, calls=%fused_computation.16.clone.1 | convolution fusion | flops 79085568 | bytes 7417860 | tf_op jit(solution)/shard_map/while/body/eval_jaxpr/rhjk,rkhd->rjhd/dot_general | solution.py:55
  126.5 3.1 %copy.30 = f32[48,48,128]{2,1,0:T(8,128)} copy(f32[48,48,128]{1,2,0:T(8,128)} %bitcast.85) | data formatting | bytes 2359296 | tf_op jit(solution)/shard_map/reshape | solution.py:37
  129.9 2.0 %copy.31 = f32[48,48,128]{2,1,0:T(8,128)} copy(f32[48,48,128]{1,2,0:T(8,128)S(1)} %bitcast.84) | data formatting | bytes 2359296 | tf_op jit(solution)/shard_map/div | solution.py:96
  131.9 3.3 %convolution_convert_fusion.2 = bf16[48,48,128]{2,1,0:T(8,128)(2,1)} fusion(bf16[48,48,128]{2,1,0:T(8,128)(2,1)} %fusion.37, f32[48,48,128]{2,1,0:T(8,128)} %copy.30, f32[48,48,128]{2,1,0:T(8,128)} %copy.31, bf16[128,128]{1,0:T(8,128)(2,1)S(1)} %copy-done.6, bf16[128,128]{1,0:T(8,128)(2,1)S(1)} %copy-done.7), kind=kOutput, calls=%fused_computation.38 | convolution fusion | flops 153059328 | bytes 3604480 | tf_op jit(solution)/shard_map/dot_general | solution.py:99
  (74 shorter events, 22.4 us)
Async XLA Ops:
  6.5 29.1 %copy-start = (bf16[128,128]{1,0:T(8,128)(2,1)S(1)}, bf16[128,128]{1,0:T(8,128)(2,1)}, u32[]{:S(2)}) copy-start(bf16[128,128]{1,0:T(8,128)(2,1)} %param.12) | copy-start | bytes 98308
  6.5 3.3 %copy-start.1 = (bf16[48,48,128]{2,1,0:T(8,128)(2,1)S(1)}, bf16[48,48,128]{2,1,0:T(8,128)(2,1)}, u32[]{:S(2)}) copy-start(bf16[48,48,128]{2,1,0:T(8,128)(2,1)} %param.10) | copy-start | bytes 1769476
  6.5 5.6 %copy-start.4 = (bf16[128,128]{1,0:T(8,128)(2,1)S(1)}, bf16[128,128]{1,0:T(8,128)(2,1)}, u32[]{:S(2)}) copy-start(bf16[128,128]{1,0:T(8,128)(2,1)} %param.13) | copy-start | bytes 98308
  6.5 5.7 %copy-start.3 = (bf16[4,48,48]{2,1,0:T(8,128)(2,1)S(1)}, bf16[4,48,48]{2,1,0:T(8,128)(2,1)}, u32[]{:S(2)}) copy-start(bf16[4,48,48]{2,1,0:T(8,128)(2,1)} %param.17) | copy-start | bytes 55300
  6.5 70.7 %all-gather.2.cloned.1.call-start = ((), (), s32[]{:S(2)}) async-start(), calls=%async_computation | async-start | bytes 10027008 | tf_op jit(solution)/shard_map/all_gather | solution.py:80
  12.1 23.4 %copy-start.5 = (bf16[128,128]{1,0:T(8,128)(2,1)S(1)}, bf16[128,128]{1,0:T(8,128)(2,1)}, u32[]{:S(2)}) copy-start(bf16[128,128]{1,0:T(8,128)(2,1)} %param.14) | copy-start | bytes 98308
  12.1 23.5 %copy-start.2 = (bf16[48,48,128]{2,1,0:T(8,128)(2,1)S(1)}, bf16[48,48,128]{2,1,0:T(8,128)(2,1)}, u32[]{:S(2)}) copy-start(bf16[48,48,128]{2,1,0:T(8,128)(2,1)} %fusion.37) | copy-start | bytes 1769476
  129.9 2.0 %copy-start.6 = (bf16[128,128]{1,0:T(8,128)(2,1)S(1)}, bf16[128,128]{1,0:T(8,128)(2,1)}, u32[]{:S(2)}) copy-start(bf16[128,128]{1,0:T(8,128)(2,1)} %param.16) | copy-start | bytes 98308
  129.9 2.0 %copy-start.7 = (bf16[128,128]{1,0:T(8,128)(2,1)S(1)}, bf16[128,128]{1,0:T(8,128)(2,1)}, u32[]{:S(2)}) copy-start(bf16[128,128]{1,0:T(8,128)(2,1)} %param.15) | copy-start | bytes 98308
Sparse Core Ops, SparseCore 0:
  12.2 64.9 all-gather.1
where the time goes:
time: 143 us; the launch traced here: 142 us
  matrix products  44.6 us (31%)
  waiting for transfers between devices  41.3 us (29%)
  blocking collectives  22.6 us (16%)
  between operations  13.5 us (9%)
  other arithmetic  12.3 us (9%)
  local copies, waits for them, and re-layouts  7.34 us (5%)
    all_gather x1, waiting for transfers between devices, body(): piece = lax.all_gather(normed, 'keys', axis=1, tiled=True)  41.3 us
    all_gather x2, blocking collectives, gathered_by_axis(): out = lax.all_gather(out, axes[number], axis=dim, tiled=True)  22.6 us
    dot_general x6, matrix products, one_block(): jnp.dot(input_block, w_value, preferred_element_type=jnp.float32)  11.9 us
    dot_general x6, matrix products, one_block(): jnp.dot(input_block, w_key, preferred_element_type=jnp.float32)  11.9 us
    dot_general x6, matrix products, absorb(): jnp.einsum('rhjk,rkhd->rjhd', powers.astype(jnp.bfloat16), split_heads(va...  11.2 us
    reduce_sum x6, other arithmetic, absorb(): totals = totals * shrink + jnp.sum(powers, axis=3)  6.3 us
    dot_general x6, matrix products, absorb(): jnp.einsum('rjhd,rkhd->rhjk', split_heads(query_block, head_count), split...  5.99 us
    dot_general x1, matrix products, body(): jnp.dot(gated, w_out, preferred_element_type=jnp.float32)  3.32 us
  transfers between devices with their start and end apart: 1, of which 1 were waited for; matrix products, arithmetic and copies ran while one was open for 1% of the time, Pallas kernels for 0%

commit v1 on v0

v1 whole, which is shorter than its diff:
```python
import functools
import math

import jax
import jax.numpy as jnp
from jax import lax
from jax.experimental import pallas as pl
from jax.experimental.pallas import tpu as pltpu
from jax.sharding import Mesh
from jax.sharding import PartitionSpec as P

AXES = ("y", "x", "z", "c")
MESH = pl.DeviceIdType.MESH
BF16, F32 = jnp.bfloat16, jnp.float32
NY, NX, NZ, NC = 4, 4, 8, 2
HEADS, DIM, CH = 4, 32, 128
BLK = 48
OWN = BLK // NZ
QRY = NZ * BLK
KEYS = NC * QRY
LANES = 128
CHUNKS = QRY // LANES
EPS = 1e-05
LOG2E = math.log2(math.e)
Z_ORDER = (4, 3, 5, 2, 6, 1, 7)
NT = (((1,), (1,)), ((), ()))
DONE = ((0, 1), (2, 3, 4), (5, 6, 7))


def dot(a, b):
    return jnp.dot(a, b, preferred_element_type=F32)


def dot_nt(a, b):
    return lax.dot_general(a, b, NT, preferred_element_type=F32)


def kernel(
    x_hbm, gain, w_query, w_key, w_value, w_gate, w_out, pair_bias, out_hbm,
    xbuf, zbias, bias, bias32, keys, values, queries, gates, wq_t, wv_t, wg_t, outbuf,
    zs, zr, as_, ar, bs, br, xs, xr, xl, fs, fr, os_, or_, ol,
):
    y, x, z, c = (lax.axis_index(a) for a in AXES)
    at = {"x": x, "y": y}

    def remote(src, dst, send, recv, **where):
        return pltpu.make_async_remote_copy(
            src_ref=src, dst_ref=dst, send_sem=send, recv_sem=recv, device_id=where, device_id_type=MESH
        )

    def wait(ref, sem):
        pltpu.make_async_copy(ref, ref, sem).wait()

    barrier = pltpu.get_barrier_semaphore()
    peers = [{"z": lax.rem(z + k, NZ)} for k in range(1, NZ)]
    peers += [{a: lax.rem(at[a] + k, 4)} for a in "xy" for k in range(1, 4)]
    peers += [{"c": 1 - c}]
    for peer in peers:
        pl.semaphore_signal(barrier, inc=1, device_id=peer, device_id_type=MESH)

    own_rows = pltpu.make_async_copy(x_hbm.at[pl.ds(z * OWN, OWN)], xbuf.at[:, 0, z], xl)
    own_rows.start()

    for g in range(2):
        packed = jnp.zeros((BLK, LANES), F32)
        for hh in range(2):
            row = lax.broadcasted_iota(jnp.int32, (BLK, LANES), 0)
            lane = lax.broadcasted_iota(jnp.int32, (BLK, LANES), 1)
            place = jnp.where(lane == row + BLK * hh, 1.0, 0.0).astype(BF16)
            packed = packed + dot(pair_bias[2 * g + hh], place)
        zbias[z, g] = packed.astype(BF16)
    for src, dst in ((w_query, wq_t), (w_value, wv_t), (w_gate, wg_t)):
        dst[...] = jnp.transpose(src[...].astype(F32)).astype(BF16)
    values[:, :, 2 * DIM :, :] = jnp.ones((OWN, 2, 16, KEYS), BF16)

    pl.semaphore_wait(barrier, len(peers))

    for k in Z_ORDER:
        remote(zbias.at[z], zbias.at[z], zs, zr, z=lax.rem(z + k, NZ)).start()

    def send_row(i, _):
        for k in Z_ORDER:
            t = lax.rem(z + k, NZ)
            remote(x_hbm.at[t * OWN + i], xbuf.at[i, 0, z], xs, xr.at[i], z=t).start()
        return 0

    lax.fori_loop(0, OWN, send_row, 0)

    wait(zbias.at[pl.ds(0, NZ - 1)], zr)
    o = jnp.where(lax.rem(x, 2) == c, 0, 1)
    x2 = x // 2
    for g in range(2):
        block = zbias[:, g].reshape(QRY, LANES)
        for hh in range(2):
            row = lax.broadcasted_iota(jnp.int32, (BLK, LANES), 0)
            lane = lax.broadcasted_iota(jnp.int32, (BLK, LANES), 1)
            place = jnp.where(lane == row + BLK * hh, 1.0, 0.0).astype(BF16)
            part = dot_nt(place, block).astype(BF16)
            for t in range(CHUNKS):
                bias[t, 2 * g + hh, o, y, x2] = part[:, LANES * t : LANES * (t + 1)]
    for t in range(CHUNKS):
        for half, axis in ((0, "x"), (1, "y")):
            mine = bias.at[t, pl.ds(2 * half, 2), o, y, x2]
            for k in (2, 1, 3):
                there = lax.rem(at[axis] + k, 4)
                remote(mine, mine, as_, ar.at[t, half], **{axis: there}).start()
    for t in range(CHUNKS):
        for half, axis in ((0, "y"), (1, "x")):
            wait(bias.at[t, pl.ds(0, 2), 0, pl.ds(0, 3), 0], ar.at[t, half])
            if half == 0:
                line = bias.at[t, pl.ds(0, 2), :, y]
            else:
                line = bias.at[t, pl.ds(2, 2), o, :, x2]
            for k in (2, 1, 3):
                there = lax.rem(at[axis] + k, 4)
                remote(line, line, bs, br.at[t, half], **{axis: there}).start()

    def normed(i, side):
        v = xbuf[i, side].reshape(QRY, CH).astype(F32)
        v = v - jnp.mean(v, axis=-1, keepdims=True)
        spread = jnp.mean(jnp.square(v), axis=-1, keepdims=True)
        return (v * lax.rsqrt(spread + EPS) * gain[...]).astype(BF16)

    def project(i, side, n):
        cols = pl.ds(side * QRY, QRY)
        keys[i, cols, :] = dot(n, w_key[...]).astype(BF16)
        v = dot_nt(wv_t[...], n).astype(BF16)
        values[i, 0, : 2 * DIM, cols] = v[: 2 * DIM]
        values[i, 1, : 2 * DIM, cols] = v[2 * DIM :]

    own_rows.wait()

    def own_side(i, _):
        wait(xbuf.at[i, 0, pl.ds(0, NZ - 1)], xr.at[i])
        remote(xbuf.at[i, 0], xbuf.at[i, 1], fs, fr.at[i], c=1 - c).start()
        n = normed(i, 0)
        project(i, 0, n)
        queries[i] = (dot_nt(wq_t[...], n) * (DIM**-0.5 * LOG2E)).astype(BF16)
        gates[i] = jax.nn.sigmoid(dot_nt(wg_t[...], n))
        return 0

    lax.fori_loop(0, OWN, own_side, 0)

    def other_side(i, _):
        wait(xbuf.at[i, 1], fr.at[i])
        project(i, 1, normed(i, 1))
        return 0

    lax.fori_loop(0, OWN, other_side, 0)

    for t in range(CHUNKS):
        lanes = slice(LANES * t, LANES * (t + 1))
        for half in range(2):
            wait(bias.at[t, pl.ds(0, 2), :, pl.ds(0, 3)], br.at[t, half])
        for h in range(HEADS):
            bias32[h // 2, :, LANES * (h % 2) : LANES * (h % 2 + 1)] = (
                bias[t, h].reshape(KEYS, LANES).astype(F32) * LOG2E
            )

        def attend(i, _):
            q = queries[i, :, lanes]
            head = lax.broadcasted_iota(jnp.int32, (CH, LANES), 0) // DIM
            rows = []
            for g in range(2):
                zero = jnp.zeros_like(q)
                rhs = jnp.concatenate([jnp.where(head == 2 * g + hh, q, zero) for hh in range(2)], axis=1)
                s = dot(keys[i], rhs) + bias32[g]
                p = jnp.exp2(s - jnp.max(s, axis=0, keepdims=True)).astype(BF16)
                sums = dot(values[i, g], p)
                for hh in range(2):
                    side = slice(LANES * hh, LANES * (hh + 1))
                    rows.append(sums[DIM * hh : DIM * (hh + 1), side] / sums[2 * DIM : 2 * DIM + 1, side])
            gated = jnp.concatenate(rows, axis=0) * gates[i, :, lanes]
            gated = jnp.transpose(gated).astype(BF16)
            outbuf[i, lanes, :] = dot(gated, w_out[...]).astype(BF16)
            for b in DONE[t]:
                done = outbuf.at[i, pl.ds(BLK * b, BLK)]

                @pl.when(z != b)
                def _():
                    remote(done, out_hbm.at[z * OWN + i], os_, or_, z=b).start()

                @pl.when(z == b)
                def _():
                    pltpu.make_async_copy(done, out_hbm.at[z * OWN + i], ol).start()

            return 0

        lax.fori_loop(0, OWN, attend, 0)

    wait(out_hbm.at[pl.ds(0, OWN * (NZ - 1))], or_)
    wait(out_hbm.at[pl.ds(0, OWN * (NZ - 1))], os_)
    wait(out_hbm.at[pl.ds(0, OWN)], ol)
    wait(zbias.at[pl.ds(0, NZ - 1)], zs)
    wait(x_hbm.at[pl.ds(0, OWN * (NZ - 1))], xs)
    wait(xbuf.at[:, 0], fs)
    for t in range(CHUNKS):
        for half in range(2):
            wait(bias.at[t, pl.ds(0, 2), 0, pl.ds(0, 3), 0], as_)
            wait(bias.at[t, pl.ds(0, 2), :, pl.ds(0, 3)], bs)


def body(pair_rep, norm_gain, w_query, w_key, w_value, w_gate, w_out, pair_bias):
    vmem = pl.BlockSpec(memory_space=pltpu.VMEM)
    anywhere = pl.BlockSpec(memory_space=pl.ANY)
    dma = pltpu.SemaphoreType.DMA
    return pl.pallas_call(
        kernel,
        out_shape=jax.ShapeDtypeStruct((BLK, BLK, CH), BF16),
        in_specs=[anywhere] + [vmem] * 7,
        out_specs=anywhere,
        scratch_shapes=[
            pltpu.VMEM((OWN, 2, NZ, BLK, CH), BF16),
            pltpu.VMEM((NZ, 2, BLK, LANES), BF16),
            pltpu.VMEM((CHUNKS, HEADS, 2, NY, NX // 2, BLK, LANES), BF16),
            pltpu.VMEM((2, KEYS, 2 * LANES), F32),
            pltpu.VMEM((OWN, KEYS, CH), BF16),
            pltpu.VMEM((OWN, 2, 2 * DIM + 16, KEYS), BF16),
            pltpu.VMEM((OWN, CH, QRY), BF16),
            pltpu.VMEM((OWN, CH, QRY), F32),
            pltpu.VMEM((CH, CH), BF16),
            pltpu.VMEM((CH, CH), BF16),
            pltpu.VMEM((CH, CH), BF16),
            pltpu.VMEM((OWN, QRY, CH), BF16),
            dma, dma,
            dma, dma((CHUNKS, 2)),
            dma, dma((CHUNKS, 2)),
            dma, dma((OWN,)), dma,
            dma, dma((OWN,)),
            dma, dma, dma,
        ],
        compiler_params=pltpu.CompilerParams(
            collective_id=0, has_side_effects=True, vmem_limit_bytes=56 * 1024 * 1024
        ),
        name="triangle_attention",
    )(pair_rep, norm_gain.reshape(1, CH), w_query, w_key, w_value, w_gate, w_out, pair_bias)


def solution(mesh):
    torus = Mesh(mesh.devices.reshape(NY, NX, NZ, NC), AXES)
    rows, cols = ("y", "x"), ("z", "c")
    placed = (P(rows, cols, None), P(), P(), P(), P(), P(), P(), P(None, cols, rows))
    return jax.shard_map(body, mesh=torus, in_specs=placed, out_specs=P(rows, cols, None), check_vma=False)
```

time: 143 us -> 62.8 us (0.44)
  Pallas kernels: 0 us -> 60.7 us
  matrix products: 44.6 us -> 0 us
  waiting for transfers between devices: 41.3 us -> 0 us
  blocking collectives: 22.6 us -> 0 us
  between operations: 13.5 us -> 0.01 us
  other arithmetic: 12.3 us -> 0 us
  local copies, waits for them, and re-layouts: 7.34 us -> 1.92 us
    pallas_call x0 -> x1, Pallas kernels: none -> 60.7 us  [body(): pl.pallas_call(kernel, out_shape=jax.ShapeDtypeStruct((BLK, BLK, CH), BF1...]
    dot_general x26 -> x0, matrix products: 44.6 us -> none  [the longest x6 11.9 us: one_block(): jnp.dot(input_block, w_value, preferred_element_type=jnp.float32)]
    all_gather x1 -> x0, waiting for transfers between devices: 41.3 us -> none  [body(): piece = lax.all_gather(normed, 'keys', axis=1, tiled=True)]
    all_gather x2 -> x0, blocking collectives: 22.6 us -> none  [gathered_by_axis(): out = lax.all_gather(out, axes[number], axis=dim, tiled=True)]
    reduce_sum x8 -> x0, other arithmetic: 9.56 us -> none  [the longest x6 6.3 us: absorb(): totals = totals * shrink + jnp.sum(powers, axis=3)]
    reshape x1 -> x0, local copies, waits for them, and re-layouts: 3.14 us -> none  [unblocked(): tensor.reshape((tensor.shape[0] * tensor.shape[1],) + tensor.shape[2:])]
    convert_element_type x7 -> x0, other arithmetic: 2.41 us -> none  [the longest x1 2.17 us: normalize(): ((values - center) * lax.rsqrt(spread + epsilon) * norm_gain).astype(jnp....]
    div x2 -> x0, local copies, waits for them, and re-layouts: 2.17 us -> none  [body(): attended = summed / jnp.transpose(totals, (0, 2, 1))[..., None]]
  transfers between devices with their start and end apart: 1 -> 0, of which waited for: 1 -> 0; matrix products, arithmetic and copies ran while one was open for 1% -> 0% of each run, Pallas kernels for 0% -> 0%
where the time goes in v1:
time: 62.8 us; the launch traced here: 62.6 us
  Pallas kernels  60.7 us (97%)
  local copies, waits for them, and re-layouts  1.92 us (3%)
    pallas_call x1, Pallas kernels, body(): pl.pallas_call(kernel, out_shape=jax.ShapeDtypeStruct((BLK, BLK, CH), BF1...  60.7 us
    unnamed x1, local copies, waits for them, and re-layouts  1.92 us

profile of v1, /device:TPU:1, one launch (start us, length us, event | category | flops | bytes accessed | tf_op | source)
XLA Modules:
  0.0 62.6 jit_solution(5581305031049207653)
XLA Ops:
  0.0 60.7 %triangle_attention.1 = bf16[48,48,128]{2,1,0:T(8,128)(2,1)} custom-call(bf16[48,48,128]{2,1,0:T(8,128)(2,1)} %x_hbm.1, f32[1,128]{1,0:T(1,128)} %bitcast.1, bf16[128,128]{1,0:T(8,128)(2,1)} %w_query.1, bf16[128,128]{1,0:T(8,128)(2,1)} %w_key.1, bf16[128,128]{1,0:T(8,128)(2,1)} %w_value.1, bf16[128,128]{1,0:T(8,128)(2,1)} %w_gate.1, bf16[128,128]{1,0:T(8,128)(2,1)} %w_out.1, ...), custom_call_target="tpu_custom_call" | custom-call | tf_op jit(solution)/shard_map/triangle_attention/pallas_call | solution.py:207
  60.7 1.9 %copy.10 = bf16[48,48,128]{2,1,0:T(8,128)(2,1)} copy(bf16[48,48,128]{2,1,0:T(8,128)(2,1)} %triangle_attention.1) | data formatting | bytes 1179648

commit v2 on v1

--- a/solution.py
+++ b/solution.py
@@ -21,9 +21,12 @@
 LANES = 128
 CHUNKS = QRY // LANES
 EPS = 1e-05
+STEP = 128
 LOG2E = math.log2(math.e)
 Z_ORDER = (4, 3, 5, 2, 6, 1, 7)
 NT = (((1,), (1,)), ((), ()))
+OFFSETS = (3, 5, 4, 2, 6, 1, 7, 0)
+PLACE = tuple(OFFSETS.index(d) for d in range(8))
 DONE = ((0, 1), (2, 3, 4), (5, 6, 7))
 
 
@@ -37,7 +40,7 @@
 
 def kernel(
     x_hbm, gain, w_query, w_key, w_value, w_gate, w_out, pair_bias, out_hbm,
-    xbuf, zbias, bias, bias32, keys, values, queries, gates, wq_t, wv_t, wg_t, outbuf,
+    xbuf, zbias, bias, bias32, keys, values, queries, gates, wq_t, wv_t, wg_t, outbuf, s0, s1, top0, top1,
     zs, zr, as_, ar, bs, br, xs, xr, xl, fs, fr, os_, or_, ol,
 ):
     y, x, z, c = (lax.axis_index(a) for a in AXES)
@@ -58,7 +61,7 @@
     for peer in peers:
         pl.semaphore_signal(barrier, inc=1, device_id=peer, device_id_type=MESH)
 
-    own_rows = pltpu.make_async_copy(x_hbm.at[pl.ds(z * OWN, OWN)], xbuf.at[:, 0, z], xl)
+    own_rows = pltpu.make_async_copy(x_hbm.at[pl.ds(z * OWN, OWN)], xbuf.at[:, 0, PLACE[0]], xl)
     own_rows.start()
 
     for g in range(2):
@@ -68,7 +71,7 @@
             lane = lax.broadcasted_iota(jnp.int32, (BLK, LANES), 1)
             place = jnp.where(lane == row + BLK * hh, 1.0, 0.0).astype(BF16)
             packed = packed + dot(pair_bias[2 * g + hh], place)
-        zbias[z, g] = packed.astype(BF16)
+        zbias[PLACE[0], g] = packed.astype(BF16)
     for src, dst in ((w_query, wq_t), (w_value, wv_t), (w_gate, wg_t)):
         dst[...] = jnp.transpose(src[...].astype(F32)).astype(BF16)
     values[:, :, 2 * DIM :, :] = jnp.ones((OWN, 2, 16, KEYS), BF16)
@@ -76,12 +79,12 @@
     pl.semaphore_wait(barrier, len(peers))
 
     for k in Z_ORDER:
-        remote(zbias.at[z], zbias.at[z], zs, zr, z=lax.rem(z + k, NZ)).start()
+        remote(zbias.at[PLACE[0]], zbias.at[PLACE[NZ - k]], zs, zr, z=lax.rem(z + k, NZ)).start()
 
     def send_row(i, _):
         for k in Z_ORDER:
             t = lax.rem(z + k, NZ)
-            remote(x_hbm.at[t * OWN + i], xbuf.at[i, 0, z], xs, xr.at[i], z=t).start()
+            remote(x_hbm.at[t * OWN + i], xbuf.at[i, 0, PLACE[NZ - k]], xs, xr.at[i], z=t).start()
         return 0
 
     lax.fori_loop(0, OWN, send_row, 0)
@@ -148,42 +151,61 @@
 
     lax.fori_loop(0, OWN, other_side, 0)
 
+    place = []
+    for b in range(NZ):
+        away = lax.rem(b - z + NZ, NZ)
+        place.append(sum(jnp.where(away == d, PLACE[d], 0) for d in range(NZ)))
+
     for t in range(CHUNKS):
         lanes = slice(LANES * t, LANES * (t + 1))
         for half in range(2):
             wait(bias.at[t, pl.ds(0, 2), :, pl.ds(0, 3)], br.at[t, half])
         for h in range(HEADS):
-            bias32[h // 2, :, LANES * (h % 2) : LANES * (h % 2 + 1)] = (
-                bias[t, h].reshape(KEYS, LANES).astype(F32) * LOG2E
-            )
-
-        def attend(i, _):
+            for side in range(2):
+                for b in range(NZ):
+                    rows = pl.ds(pl.multiple_of(side * QRY + BLK * place[b], 16), BLK)
+                    bias32[h // 2, rows, LANES * (h % 2) : LANES * (h % 2 + 1)] = (
+                        bias[t, h, side, b // 2, b % 2].astype(F32) * LOG2E
+                    )
+
+        def scores(i, g, s_ref, top_ref):
             q = queries[i, :, lanes]
             head = lax.broadcasted_iota(jnp.int32, (CH, LANES), 0) // DIM
+            rhs = jnp.concatenate([jnp.where(head == 2 * g + hh, q, jnp.zeros_like(q)) for hh in range(2)], axis=1)
+            top = None
+            for k in range(0, KEYS, STEP):
+                s = dot(keys[i, k : k + STEP, :], rhs) + bias32[g, k : k + STEP, :]
+                s_ref[k : k + STEP, :] = s
+                peak = jnp.max(s.reshape(STEP // 8, 8, 2 * LANES), axis=0)
+                top = peak if top is None else jnp.maximum(top, peak)
+            top_ref[...] = top
+
+        def weigh(i, g, s_ref, top_ref):
+            top = jnp.max(top_ref[...], axis=0, keepdims=True)
+            p = [jnp.exp2(s_ref[k : k + STEP, :] - top).astype(BF16) for k in range(0, KEYS, STEP)]
+            sums = dot(values[i, g], jnp.concatenate(p, axis=0))
             rows = []
-            for g in range(2):
-                zero = jnp.zeros_like(q)
-                rhs = jnp.concatenate([jnp.where(head == 2 * g + hh, q, zero) for hh in range(2)], axis=1)
-                s = dot(keys[i], rhs) + bias32[g]
-                p = jnp.exp2(s - jnp.max(s, axis=0, keepdims=True)).astype(BF16)
-                sums = dot(values[i, g], p)
-                for hh in range(2):
-                    side = slice(LANES * hh, LANES * (hh + 1))
-                    rows.append(sums[DIM * hh : DIM * (hh + 1), side] / sums[2 * DIM : 2 * DIM + 1, side])
-            gated = jnp.concatenate(rows, axis=0) * gates[i, :, lanes]
+            for hh in range(2):
+                side = slice(LANES * hh, LANES * (hh + 1))
+                rows.append(sums[DIM * hh : DIM * (hh + 1), side] / sums[2 * DIM : 2 * DIM + 1, side])
+            return jnp.concatenate(rows, axis=0)
+
+        scores(0, 0, s0, top0)
+
+        def attend(i, _):
+            scores(i, 1, s1, top1)
+            first = weigh(i, 0, s0, top0)
+            scores(jnp.minimum(i + 1, OWN - 1), 0, s0, top0)
+            second = weigh(i, 1, s1, top1)
+            gated = jnp.concatenate([first, second], axis=0) * gates[i, :, lanes]
             gated = jnp.transpose(gated).astype(BF16)
             outbuf[i, lanes, :] = dot(gated, w_out[...]).astype(BF16)
             for b in DONE[t]:
-                done = outbuf.at[i, pl.ds(BLK * b, BLK)]
-
-                @pl.when(z != b)
-                def _():
-                    remote(done, out_hbm.at[z * OWN + i], os_, or_, z=b).start()
-
-                @pl.when(z == b)
-                def _():
-                    pltpu.make_async_copy(done, out_hbm.at[z * OWN + i], ol).start()
-
+                done, there = outbuf.at[i, pl.ds(BLK * b, BLK)], out_hbm.at[z * OWN + i]
+                if OFFSETS[b]:
+                    remote(done, there, os_, or_, z=lax.rem(z + OFFSETS[b], NZ)).start()
+                else:
+                    pltpu.make_async_copy(done, there, ol).start()
             return 0
 
         lax.fori_loop(0, OWN, attend, 0)
@@ -222,6 +244,10 @@
             pltpu.VMEM((CH, CH), BF16),
             pltpu.VMEM((CH, CH), BF16),
             pltpu.VMEM((OWN, QRY, CH), BF16),
+            pltpu.VMEM((KEYS, 2 * LANES), F32),
+            pltpu.VMEM((KEYS, 2 * LANES), F32),
+            pltpu.VMEM((8, 2 * LANES), F32),
+            pltpu.VMEM((8, 2 * LANES), F32),
             dma, dma,
             dma, dma((CHUNKS, 2)),
             dma, dma((CHUNKS, 2)),

time: 62.8 us -> 50.6 us (0.81); the launches traced: 62.6 us -> 49.8 us
  Pallas kernels: 60.7 us -> 47.9 us
    pallas_call x1, Pallas kernels: 60.7 us -> 47.9 us  [body(): pl.pallas_call(kernel, out_shape=jax.ShapeDtypeStruct((BLK, BLK, CH), BF1...]
where the time goes in v2:
time: 50.6 us; the launch traced here: 49.8 us
  Pallas kernels  47.9 us (95%)
  local copies, waits for them, and re-layouts  1.92 us (4%)
    pallas_call x1, Pallas kernels, body(): pl.pallas_call(kernel, out_shape=jax.ShapeDtypeStruct((BLK, BLK, CH), BF1...  47.9 us
    unnamed x1, local copies, waits for them, and re-layouts  1.92 us

profile of v2, /device:TPU:1, one launch (start us, length us, event | category | flops | bytes accessed | tf_op | source)
XLA Modules:
  0.0 49.8 jit_solution(14387737710413453182)
XLA Ops:
  0.0 47.9 %triangle_attention.1 = bf16[48,48,128]{2,1,0:T(8,128)(2,1)} custom-call(bf16[48,48,128]{2,1,0:T(8,128)(2,1)} %x_hbm.1, f32[1,128]{1,0:T(1,128)} %bitcast.1, bf16[128,128]{1,0:T(8,128)(2,1)} %w_query.1, bf16[128,128]{1,0:T(8,128)(2,1)} %w_key.1, bf16[128,128]{1,0:T(8,128)(2,1)} %w_value.1, bf16[128,128]{1,0:T(8,128)(2,1)} %w_gate.1, bf16[128,128]{1,0:T(8,128)(2,1)} %w_out.1, ...), custom_call_target="tpu_custom_call" | custom-call | tf_op jit(solution)/shard_map/triangle_attention/pallas_call | solution.py:229
  47.9 1.9 %copy.10 = bf16[48,48,128]{2,1,0:T(8,128)(2,1)} copy(bf16[48,48,128]{2,1,0:T(8,128)(2,1)} %triangle_attention.1) | data formatting | bytes 1179648

commit v3 on v2

--- a/solution.py
+++ b/solution.py
@@ -39,9 +39,10 @@
 
 
 def kernel(
-    x_hbm, gain, w_query, w_key, w_value, w_gate, w_out, pair_bias, out_hbm,
-    xbuf, zbias, bias, bias32, keys, values, queries, gates, wq_t, wv_t, wg_t, outbuf, s0, s1, top0, top1,
-    zs, zr, as_, ar, bs, br, xs, xr, xl, fs, fr, os_, or_, ol,
+    x_hbm, gain_hbm, w_query_hbm, w_key_hbm, w_value_hbm, w_gate_hbm, w_out_hbm, pair_bias_hbm, out_hbm,
+    gain, w_query, w_key, w_value, w_gate, w_out, pair_bias,
+    xbuf, zbias, bias, bias32, keys, values, queries, gates, wq_t, wv_t, wg_t, outbuf, s0, s1, top0, top1, result,
+    zs, zr, as_, ar, bs, br, xs, xr, xl, fs, fr, os_, or_, ol, wl,
 ):
     y, x, z, c = (lax.axis_index(a) for a in AXES)
     at = {"x": x, "y": y}
@@ -61,9 +62,20 @@
     for peer in peers:
         pl.semaphore_signal(barrier, inc=1, device_id=peer, device_id_type=MESH)
 
+    loads = [
+        pltpu.make_async_copy(src, dst, wl.at[n])
+        for n, (src, dst) in enumerate((
+            (pair_bias_hbm, pair_bias), (w_query_hbm, w_query), (w_value_hbm, w_value), (w_gate_hbm, w_gate),
+            (w_key_hbm, w_key), (w_out_hbm, w_out), (gain_hbm, gain),
+        ))
+    ]
+    for load in loads:
+        load.start()
     own_rows = pltpu.make_async_copy(x_hbm.at[pl.ds(z * OWN, OWN)], xbuf.at[:, 0, PLACE[0]], xl)
     own_rows.start()
 
+    for load in loads:
+        load.wait()
     for g in range(2):
         packed = jnp.zeros((BLK, LANES), F32)
         for hh in range(2):
@@ -75,6 +87,8 @@
     for src, dst in ((w_query, wq_t), (w_value, wv_t), (w_gate, wg_t)):
         dst[...] = jnp.transpose(src[...].astype(F32)).astype(BF16)
     values[:, :, 2 * DIM :, :] = jnp.ones((OWN, 2, 16, KEYS), BF16)
+
+    result[...] = jnp.zeros_like(result)
 
     pl.semaphore_wait(barrier, len(peers))
 
@@ -133,23 +147,35 @@
 
     own_rows.wait()
 
-    def own_side(i, _):
+    def own_here(i):
         wait(xbuf.at[i, 0, pl.ds(0, NZ - 1)], xr.at[i])
         remote(xbuf.at[i, 0], xbuf.at[i, 1], fs, fr.at[i], c=1 - c).start()
+
+    def own_side(i):
         n = normed(i, 0)
         project(i, 0, n)
         queries[i] = (dot_nt(wq_t[...], n) * (DIM**-0.5 * LOG2E)).astype(BF16)
         gates[i] = jax.nn.sigmoid(dot_nt(wg_t[...], n))
+
+    def other_here(i):
+        wait(xbuf.at[i, 1], fr.at[i])
+
+    def other_side(i):
+        project(i, 1, normed(i, 1))
+
+    own_here(0)
+    own_side(0)
+
+    def prepare(i, _):
+        own_here(i + 1)
+        other_here(i)
+        own_side(i + 1)
+        other_side(i)
         return 0
 
-    lax.fori_loop(0, OWN, own_side, 0)
-
-    def other_side(i, _):
-        wait(xbuf.at[i, 1], fr.at[i])
-        project(i, 1, normed(i, 1))
-        return 0
-
-    lax.fori_loop(0, OWN, other_side, 0)
+    lax.fori_loop(0, OWN - 1, prepare, 0)
+    other_here(OWN - 1)
+    other_side(OWN - 1)
 
     place = []
     for b in range(NZ):
@@ -192,23 +218,31 @@
 
         scores(0, 0, s0, top0)
 
-        def attend(i, _):
-            scores(i, 1, s1, top1)
-            first = weigh(i, 0, s0, top0)
-            scores(jnp.minimum(i + 1, OWN - 1), 0, s0, top0)
-            second = weigh(i, 1, s1, top1)
-            gated = jnp.concatenate([first, second], axis=0) * gates[i, :, lanes]
-            gated = jnp.transpose(gated).astype(BF16)
+        def finish(i):
+            gated = jnp.transpose(result[...]).astype(BF16)
             outbuf[i, lanes, :] = dot(gated, w_out[...]).astype(BF16)
+
+        def send(i):
             for b in DONE[t]:
                 done, there = outbuf.at[i, pl.ds(BLK * b, BLK)], out_hbm.at[z * OWN + i]
                 if OFFSETS[b]:
                     remote(done, there, os_, or_, z=lax.rem(z + OFFSETS[b], NZ)).start()
                 else:
                     pltpu.make_async_copy(done, there, ol).start()
+
+        def attend(i, _):
+            finish(jnp.maximum(i - 1, 0))
+            scores(i, 1, s1, top1)
+            first = weigh(i, 0, s0, top0)
+            scores(jnp.minimum(i + 1, OWN - 1), 0, s0, top0)
+            second = weigh(i, 1, s1, top1)
+            result[...] = jnp.concatenate([first, second], axis=0) * gates[i, :, lanes]
+            pl.when(i > 0)(lambda: send(i - 1))
             return 0
 
         lax.fori_loop(0, OWN, attend, 0)
+        finish(OWN - 1)
+        send(OWN - 1)
 
     wait(out_hbm.at[pl.ds(0, OWN * (NZ - 1))], or_)
     wait(out_hbm.at[pl.ds(0, OWN * (NZ - 1))], os_)
@@ -223,15 +257,17 @@
 
 
 def body(pair_rep, norm_gain, w_query, w_key, w_value, w_gate, w_out, pair_bias):
-    vmem = pl.BlockSpec(memory_space=pltpu.VMEM)
     anywhere = pl.BlockSpec(memory_space=pl.ANY)
     dma = pltpu.SemaphoreType.DMA
     return pl.pallas_call(
         kernel,
         out_shape=jax.ShapeDtypeStruct((BLK, BLK, CH), BF16),
-        in_specs=[anywhere] + [vmem] * 7,
+        in_specs=[anywhere] * 8,
         out_specs=anywhere,
         scratch_shapes=[
+            pltpu.VMEM((1, CH), F32),
+            *[pltpu.VMEM((CH, CH), BF16)] * 5,
+            pltpu.VMEM((HEADS, BLK, BLK), BF16),
             pltpu.VMEM((OWN, 2, NZ, BLK, CH), BF16),
             pltpu.VMEM((NZ, 2, BLK, LANES), BF16),
             pltpu.VMEM((CHUNKS, HEADS, 2, NY, NX // 2, BLK, LANES), BF16),
@@ -248,12 +284,14 @@
             pltpu.VMEM((KEYS, 2 * LANES), F32),
             pltpu.VMEM((8, 2 * LANES), F32),
             pltpu.VMEM((8, 2 * LANES), F32),
+            pltpu.VMEM((CH, LANES), F32),
             dma, dma,
             dma, dma((CHUNKS, 2)),
             dma, dma((CHUNKS, 2)),
             dma, dma((OWN,)), dma,
             dma, dma((OWN,)),
             dma, dma, dma,
+            dma((7,)),
         ],
         compiler_params=pltpu.CompilerParams(
             collective_id=0, has_side_effects=True, vmem_limit_bytes=56 * 1024 * 1024

time: 50.6 us -> 48.9 us (0.966); the launches traced: 49.8 us -> 48.8 us
  Pallas kernels: 47.9 us -> 46.8 us
    pallas_call x1, Pallas kernels: 47.9 us -> 46.8 us  [body(): pl.pallas_call(kernel, out_shape=jax.ShapeDtypeStruct((BLK, BLK, CH), BF1...]
where the time goes in v3:
time: 48.9 us; the launch traced here: 48.8 us
  Pallas kernels  46.8 us (96%)
  local copies, waits for them, and re-layouts  1.92 us (4%)
    pallas_call x1, Pallas kernels, body(): pl.pallas_call(kernel, out_shape=jax.ShapeDtypeStruct((BLK, BLK, CH), BF1...  46.8 us
    unnamed x1, local copies, waits for them, and re-layouts  1.92 us

profile of v3, /device:TPU:1, one launch (start us, length us, event | category | flops | bytes accessed | tf_op | source)
XLA Modules:
  0.0 48.8 jit_solution(10517003918920328431)
XLA Ops:
  0.0 46.8 %triangle_attention.1 = bf16[48,48,128]{2,1,0:T(8,128)(2,1)} custom-call(bf16[48,48,128]{2,1,0:T(8,128)(2,1)} %x_hbm.1, f32[1,128]{1,0:T(1,128)} %bitcast.1, bf16[128,128]{1,0:T(8,128)(2,1)} %w_query_hbm.1, bf16[128,128]{1,0:T(8,128)(2,1)} %w_key_hbm.1, bf16[128,128]{1,0:T(8,128)(2,1)} %w_value_hbm.1, bf16[128,128]{1,0:T(8,128)(2,1)} %w_gate_hbm.1, ...), custom_call_target="tpu_custom_call" | custom-call | tf_op jit(solution)/shard_map/triangle_attention/pallas_call | solution.py:262
  46.9 1.9 %copy.10 = bf16[48,48,128]{2,1,0:T(8,128)(2,1)} copy(bf16[48,48,128]{2,1,0:T(8,128)(2,1)} %triangle_attention.1) | data formatting | bytes 1179648
